TPU v7x, 512 devices: a whole 4x4x16 slice. The times are simulated.
512 devices in a mesh: len: 128 (over y, z, core), pipe: 4 (over x).
Axes of the slice: x: 4, y: 4, z: 16, core: 2. Of those that a mesh axis runs over, the one named last changes fastest.
Arguments:
- inputs: bfloat16 [512, 2048, 256], P(('len', 'pipe')), may hold values from -6 to 6
- cotangent: bfloat16 [512, 2048, 256], P(('len', 'pipe')), may hold values from -6 to 6
- point_weight: bfloat16 [256, 256], replicated, may hold values from -0.375 to 0.375
- point_bias: float32 [256], replicated, may hold values from -3 to 3
- spec_real: bfloat16 [128, 256, 256], P('len'), may hold values from -0.25 to 0.25
- spec_imag: bfloat16 [128, 256, 256], P('len'), may hold values from -0.25 to 0.25
- junc_weight: bfloat16 [256, 256], replicated, may hold values from -0.375 to 0.375
- junc_bias: float32 [256], replicated, may hold values from -3 to 3
- inlet_ids: int32 [512], replicated, may hold values from 0 to 511
- outlet_ids: int32 [512], replicated, may hold values from 0 to 511
Outputs:
- outputs: bfloat16 [512, 2048, 256], P(('len', 'pipe'))
- grad_inputs: bfloat16 [512, 2048, 256], P(('len', 'pipe'))
- grad_real: float32 [128, 256, 256], P('len')
- grad_imag: float32 [128, 256, 256], P('len')
All inputs are finite; a program needn't handle non-finite values.
Results may differ from a plain program's by a relative error of at most 0.015.
Values may be sent and summed in bfloat16 or wider, within the bound.
A program may use at most 64 MiB of HBM per device.

v0:
```python
import math
import jax
import jax.numpy as jnp
from jax import lax
from jax.sharding import PartitionSpec as P

COUPLING = 0.125


def tables(cell_count, mode_count):
    position = lax.broadcasted_iota(jnp.int32, (mode_count, cell_count), 1)
    frequency = lax.broadcasted_iota(jnp.int32, (mode_count, cell_count), 0)
    product_index = frequency * position % cell_count
    angles = product_index.astype(jnp.float32) * (2.0 * math.pi / cell_count)
    norm_scale = 1.0 / math.sqrt(cell_count)
    cosine = jnp.cos(angles) * norm_scale
    sine_table = jnp.sin(angles) * norm_scale
    doubled = jnp.where(frequency == 0, 1.0, 2.0)
    forward = (
        jnp.stack([cosine, -sine_table], axis=1)
        .reshape(2 * mode_count, cell_count)
        .astype(jnp.bfloat16)
    )
    inverse = jnp.transpose(
        jnp.stack([doubled * cosine, -doubled * sine_table], axis=1).reshape(
            2 * mode_count, cell_count
        )
    ).astype(jnp.bfloat16)
    return (forward, inverse)


def spectral_blocks(spec_real, spec_imag):
    upper = jnp.concatenate([spec_real, spec_imag], axis=2)
    lower = jnp.concatenate([-spec_imag, spec_real], axis=2)
    return jnp.concatenate([upper, lower], axis=1)


def activate(values):
    return jax.nn.gelu(values, approximate=True)


def silu_slope(values):
    sigmoid_part = jax.nn.sigmoid(values)
    return sigmoid_part * (1.0 + values * (1.0 - sigmoid_part))


def to_modes(field):
    return lax.all_to_all(field, "len", split_axis=1, concat_axis=0, tiled=True)


def from_modes(field):
    return lax.all_to_all(field, "len", split_axis=0, concat_axis=1, tiled=True)


def junction_pass(partial_value, rowwise, carried):
    summed_rows = lax.psum(partial_value, ("len", "pipe"))
    return rowwise(summed_rows, carried)


def body(
    inputs,
    cotangent,
    point_weight,
    point_bias,
    spec_real,
    spec_imag,
    junc_weight,
    junc_bias,
    inlet_ids,
    outlet_ids,
):
    per_dev, cell_count, channels = inputs.shape
    len_count = lax.axis_size("len")
    mode_count = spec_real.shape[0] * len_count
    junc_count = inlet_ids.shape[0]
    forward, inverse = tables(cell_count, mode_count)
    blocks = spectral_blocks(spec_real, spec_imag)
    start = (lax.axis_index("len") * lax.axis_size("pipe") + lax.axis_index("pipe")) * per_dev
    my_inlets = lax.dynamic_slice_in_dim(inlet_ids, start, per_dev)
    my_outlets = lax.dynamic_slice_in_dim(outlet_ids, start, per_dev)
    junction_iota = lax.broadcasted_iota(jnp.int32, (per_dev, junc_count), 1)
    in_hot = (my_inlets[:, None] == junction_iota).astype(jnp.bfloat16)
    out_hot = (my_outlets[:, None] == junction_iota).astype(jnp.bfloat16)
    spectra = jnp.einsum("kl,plc->pkc", forward, inputs, preferred_element_type=jnp.float32).astype(
        jnp.bfloat16
    )
    mode_rows = to_modes(spectra.reshape(per_dev, mode_count, 2, channels))
    mode_rows = mode_rows.reshape(mode_rows.shape[0], -1, 2 * channels)
    mixed = jnp.einsum(
        "pmk,mkn->pmn", mode_rows, blocks, preferred_element_type=jnp.float32
    ).astype(jnp.bfloat16)
    returned_modes = from_modes(mixed.reshape(mixed.shape[0], -1, 2, channels)).reshape(
        per_dev, 2 * mode_count, channels
    )

    def forward_rows(summed_rows, carried):
        junc_act = (
            jnp.dot(
                summed_rows.astype(jnp.bfloat16), junc_weight, preferred_element_type=jnp.float32
            )
            + junc_bias
        )
        return (jax.nn.silu(junc_act).astype(jnp.bfloat16), junc_act)

    def backward_rows(summed_rows, carried):
        act_grad = (summed_rows * silu_slope(carried)).astype(jnp.bfloat16)
        return (
            jnp.dot(act_grad, junc_weight.T, preferred_element_type=jnp.float32).astype(
                jnp.bfloat16
            ),
            carried,
        )

    partial_value = jnp.dot(
        in_hot.T, inputs[:, 0, :], preferred_element_type=jnp.float32
    ) + jnp.dot(out_hot.T, inputs[:, -1, :], preferred_element_type=jnp.float32)
    junc_rows, junc_act = junction_pass(partial_value, forward_rows, None)
    cond = COUPLING * (
        jnp.dot(in_hot, junc_rows, preferred_element_type=jnp.float32)
        + jnp.dot(out_hot, junc_rows, preferred_element_type=jnp.float32)
    )
    spectral = jnp.einsum(
        "lk,pkc->plc", inverse, returned_modes, preferred_element_type=jnp.float32
    )
    pre = (spectral + cond[:, None, :]).astype(jnp.bfloat16)
    pointwise = jnp.dot(
        inputs.reshape(-1, channels), point_weight, preferred_element_type=jnp.float32
    ).reshape(inputs.shape)
    summed = pointwise + point_bias + pre.astype(jnp.float32)
    result, pullback = jax.vjp(activate, summed)
    outputs = result.astype(jnp.bfloat16)
    grad_total = pullback(cotangent.astype(jnp.float32))[0].astype(jnp.bfloat16)
    grad_spec = jnp.einsum(
        "lk,plc->pkc", inverse, grad_total, preferred_element_type=jnp.float32
    ).astype(jnp.bfloat16)
    grad_modes = to_modes(grad_spec.reshape(per_dev, mode_count, 2, channels))
    grad_modes = grad_modes.reshape(grad_modes.shape[0], -1, 2 * channels)
    grad_mixed = jnp.einsum(
        "pmn,mkn->pmk", grad_modes, blocks, preferred_element_type=jnp.float32
    ).astype(jnp.bfloat16)
    weight_terms = jnp.einsum(
        "pmk,pmn->mkn", mode_rows, grad_modes, preferred_element_type=jnp.float32
    )
    real_terms = weight_terms[:, :channels, :channels] + weight_terms[:, channels:, channels:]
    imag_terms = weight_terms[:, :channels, channels:] - weight_terms[:, channels:, :channels]
    grad_real, grad_imag = (
        lax.psum(real_terms.astype(jnp.bfloat16), "pipe").astype(jnp.float32),
        lax.psum(imag_terms.astype(jnp.bfloat16), "pipe").astype(jnp.float32),
    )
    grad_back = from_modes(grad_mixed.reshape(grad_mixed.shape[0], -1, 2, channels)).reshape(
        per_dev, 2 * mode_count, channels
    )
    grad_cells = jnp.einsum("kl,pkc->plc", forward, grad_back, preferred_element_type=jnp.float32)
    grad_cond = jnp.sum(grad_total, axis=1, dtype=jnp.float32)
    in_wide = in_hot.astype(jnp.float32)
    out_wide = out_hot.astype(jnp.float32)
    partial_grad = COUPLING * (
        jnp.dot(in_wide.T, grad_cond, precision=lax.Precision.HIGHEST)
        + jnp.dot(out_wide.T, grad_cond, precision=lax.Precision.HIGHEST)
    )
    sums_grad, unused = junction_pass(partial_grad, backward_rows, junc_act)
    end_first = jnp.dot(in_hot, sums_grad, preferred_element_type=jnp.float32)
    end_last = jnp.dot(out_hot, sums_grad, preferred_element_type=jnp.float32)
    grad_cells = grad_cells.at[:, 0, :].add(end_first).at[:, -1, :].add(end_last)
    spread = grad_cells.astype(jnp.bfloat16)
    grad_local = jnp.dot(
        grad_total.reshape(-1, channels), point_weight.T, preferred_element_type=jnp.float32
    ).reshape(inputs.shape)
    grad_inputs = (grad_local + spread.astype(jnp.float32)).astype(jnp.bfloat16)
    return (outputs, grad_inputs, grad_real, grad_imag)


def solution(mesh):
    placed = (
        P(("len", "pipe"), None, None),
        P(("len", "pipe"), None, None),
        P(),
        P(),
        P("len", None, None),
        P("len", None, None),
        P(),
        P(),
        P(),
        P(),
    )
    return jax.shard_map(
        body,
        mesh=mesh,
        in_specs=placed,
        out_specs=(
            P(("len", "pipe"), None, None),
            P(("len", "pipe"), None, None),
            P("len", None, None),
            P("len", None, None),
        ),
        check_vma=False,
    )
```

profile of v0, /device:TPU:8, one launch (start us, length us, event | category | flops | bytes accessed | tf_op | source)
XLA Modules:
  0.0 741.6 jit_solution(12216176334191740046)
XLA Ops:
  7.2 4.3 negate_convert_fusion
  11.6 1.1 copy.32
  14.4 19.6 %all-to-all-start = ((bf16[1,128,2,256]{3,2,0,1:T(2,128)(2,1)}), bf16[1,128,2,256]{3,2,0,1:T(2,128)(2,1)S(1)}, u32[]{:S(2)}, u32[]{:S(2)}) async-start(bf16[1,128,2,256]{3,2,0,1:T(2,128)(2,1)} %bitcast.6), calls=%async_computation | async-start | bytes 262144 | tf_op jit(solution)/shard_map/all_to_all | solution.py:48
  34.0 1.3 dynamic_slice.6
  36.0 1.2 dynamic_slice.7
  38.0 106.2 %all-reduce.8 = bf16[512,256]{1,0:T(8,128)(2,1)S(1)} all-reduce(f32[512,256]{1,0:T(8,128)S(1)} %multiply_add_fusion), channel_id=1, replica_groups=mesh['len'=128,'pipe'=4] {'len','pipe'}, use_global_device_ids=true, to_apply=%region_0.1 | all-reduce | flops 131072 | bytes 786432 | tf_op jit(solution)/shard_map/psum | solution.py:56
  144.2 4.4 multiply_convert_fusion.1
  151.9 15.3 %all-to-all-start.1 = ((bf16[128,1,2,256]{3,2,1,0:T(2,128)(2,1)}), bf16[128,1,2,256]{3,2,1,0:T(2,128)(2,1)}, u32[]{:S(2)}, u32[]{:S(2)}) async-start(bf16[128,1,2,256]{3,2,1,0:T(2,128)(2,1)} %copy.34), calls=%async_computation.1 | async-start | bytes 262144 | tf_op jit(solution)/shard_map/all_to_all | solution.py:52
  169.5 14.5 %all-to-all-done.1 = bf16[128,1,2,256]{3,2,1,0:T(2,128)(2,1)} async-done(((bf16[128,1,2,256]{3,2,1,0:T(2,128)(2,1)}), bf16[128,1,2,256]{3,2,1,0:T(2,128)(2,1)}, u32[]{:S(2)}, u32[]{:S(2)}) %all-to-all-start.1) | async-done | bytes 131104 | tf_op jit(solution)/shard_map/all_to_all | solution.py:52
  186.2 3.0 convert_reduce_fusion
  191.4 7.2 all-to-all-start.2
  198.7 1.2 convert_add_fusion
  200.9 15.0 %all-to-all-done.2 = bf16[1,128,2,256]{3,2,0,1:T(2,128)(2,1)S(1)} async-done(((bf16[1,128,2,256]{3,2,0,1:T(2,128)(2,1)}), bf16[1,128,2,256]{3,2,0,1:T(2,128)(2,1)S(1)}, u32[]{:S(2)}, u32[]{:S(2)}) %all-to-all-start.2) | async-done | bytes 131104 | tf_op jit(solution)/shard_map/all_to_all | solution.py:48
  217.3 7.2 all-to-all-start.3
  225.3 439.5 %all-reduce.5.cloned.1.call-done = f32[512,256]{1,0:T(8,128)} async-done(((f32[512,256]{1,0:T(8,128)}), f32[512,256]{1,0:T(8,128)}) %all-reduce.5.cloned.1.call-update) | async-done | bytes 524304 | tf_op jit(solution)/shard_map/psum | solution.py:56
  664.8 1.4 convolution_convert_fusion
  666.4 54.7 %all-reduce.7.cloned.1.call-done = (bf16[1,256,256]{2,1,0:T(8,128)(2,1)}, bf16[1,256,256]{2,1,0:T(8,128)(2,1)}) async-done(((bf16[1,256,256]{2,1,0:T(8,128)(2,1)}, bf16[1,256,256]{2,1,0:T(8,128)(2,1)}), (bf16[1,256,256]{2,1,0:T(8,128)(2,1)}, bf16[1,256,256]{2,1,0:T(8,128)(2,1)})) %all-reduce.7.cloned.1.call-update) | async-done | bytes 262160 | tf_op jit(solution)/shard_map/psum | solution.py:147
  721.0 1.6 convert_element_type.176
  722.7 1.6 convert_element_type.178
  725.0 1.4 fusion.43
  726.5 1.8 copy.39
  728.3 1.3 scatter-add.6
  730.4 1.3 scatter-add.9
  731.8 3.0 fusion.4
  (84 shorter events, 17.9 us)
Async XLA Ops:
  7.2 178.4 %copy-start = (bf16[256,256]{1,0:T(8,128)(2,1)S(1)}, bf16[256,256]{1,0:T(8,128)(2,1)}, u32[]{:S(2)}) copy-start(bf16[256,256]{1,0:T(8,128)(2,1)} %param.16) | copy-start | bytes 393220
  11.6 1.5 copy-start.3
  13.2 135.4 %copy-start.14 = (bf16[256,256]{1,0:T(8,128)(2,1)S(1)}, bf16[256,256]{1,0:T(8,128)(2,1)}, u32[]{:S(2)}) copy-start(bf16[256,256]{1,0:T(8,128)(2,1)} %param.20) | copy-start | bytes 393220
  13.2 135.4 %copy-start.16 = (f32[256]{0:T(256)S(1)}, f32[256]{0:T(256)}, u32[]{:S(2)}) copy-start(f32[256]{0:T(256)} %param.21) | copy-start | bytes 3076
  14.4 136.3 %all-to-all-start = ((bf16[1,128,2,256]{3,2,0,1:T(2,128)(2,1)}), bf16[1,128,2,256]{3,2,0,1:T(2,128)(2,1)S(1)}, u32[]{:S(2)}, u32[]{:S(2)}) async-start(bf16[1,128,2,256]{3,2,0,1:T(2,128)(2,1)} %bitcast.6), calls=%async_computation | async-start | bytes 262144 | tf_op jit(solution)/shard_map/all_to_all | solution.py:48
  144.2 6.1 copy-start.7
  149.7 1.0 copy-start.12
  150.7 17.1 %copy-start.5 = (bf16[16,8,2,256]{3,1,2,0:T(8,128)(2,1)}, bf16[16,8,2,256]{3,1,2,0:T(8,128)(2,1)S(1)}, u32[]{:S(2)}) copy-start(bf16[16,8,2,256]{3,1,2,0:T(8,128)(2,1)S(1)} %copy.41) | copy-start | bytes 393220
  151.9 32.2 %all-to-all-start.1 = ((bf16[128,1,2,256]{3,2,1,0:T(2,128)(2,1)}), bf16[128,1,2,256]{3,2,1,0:T(2,128)(2,1)}, u32[]{:S(2)}, u32[]{:S(2)}) async-start(bf16[128,1,2,256]{3,2,1,0:T(2,128)(2,1)} %copy.34), calls=%async_computation.1 | async-start | bytes 262144 | tf_op jit(solution)/shard_map/all_to_all | solution.py:52
  169.3 16.3 %copy-start.4 = (bf16[1,2048,256]{2,1,0:T(8,128)(2,1)S(1)}, bf16[1,2048,256]{2,1,0:T(8,128)(2,1)}, u32[]{:S(2)}) copy-start(bf16[1,2048,256]{2,1,0:T(8,128)(2,1)} %param.14) | copy-start | bytes 3145732
  169.3 16.3 %copy-start.17 = (f32[256]{0:T(256)S(1)}, f32[256]{0:T(256)}, u32[]{:S(2)}) copy-start(f32[256]{0:T(256)} %param.17) | copy-start | bytes 3076
  185.0 1.2 copy-start.11
  189.2 1.0 copy-start.1
  189.2 26.6 %copy-start.8 = (bf16[1,256,256]{2,1,0:T(8,128)(2,1)S(1)}, bf16[1,256,256]{2,1,0:T(8,128)(2,1)}, u32[]{:S(2)}) copy-start(bf16[1,256,256]{2,1,0:T(8,128)(2,1)} %param.19) | copy-start | bytes 393220
  189.2 26.6 %copy-start.10 = (bf16[1,256,256]{2,1,0:T(8,128)(2,1)S(1)}, bf16[1,256,256]{2,1,0:T(8,128)(2,1)}, u32[]{:S(2)}) copy-start(bf16[1,256,256]{2,1,0:T(8,128)(2,1)} %copy-done.9) | copy-start | bytes 393220
  189.2 26.6 %copy-start.13 = (bf16[1,256,256]{2,1,0:T(8,128)(2,1)S(1)}, bf16[1,256,256]{2,1,0:T(8,128)(2,1)}, u32[]{:S(2)}) copy-start(bf16[1,256,256]{2,1,0:T(8,128)(2,1)} %param.18) | copy-start | bytes 393220
  190.7 25.5 %copy-start.6 = (bf16[16,8,2,256]{3,1,2,0:T(8,128)(2,1)S(1)}, bf16[16,8,2,256]{3,1,2,0:T(8,128)(2,1)}, u32[]{:S(2)}) copy-start(bf16[16,8,2,256]{3,1,2,0:T(8,128)(2,1)} %copy-done.5) | copy-start | bytes 393220
  191.4 24.4 %all-to-all-start.2 = ((bf16[1,128,2,256]{3,2,0,1:T(2,128)(2,1)}), bf16[1,128,2,256]{3,2,0,1:T(2,128)(2,1)S(1)}, u32[]{:S(2)}, u32[]{:S(2)}) async-start(bf16[1,128,2,256]{3,2,0,1:T(2,128)(2,1)} %bitcast.24), calls=%async_computation.2 | async-start | bytes 262144 | tf_op jit(solution)/shard_map/all_to_all | solution.py:48
  198.6 466.2 %all-reduce.5.cloned.1.call-start = ((), (), s32[]{:S(2)}) async-start(), calls=%async_computation.4 | async-start | bytes 1048576 | tf_op jit(solution)/shard_map/psum | solution.py:56
  216.2 448.6 %copy-start.15 = (bf16[256,256]{1,0:T(8,128)(2,1)S(1)}, bf16[256,256]{1,0:T(8,128)(2,1)}, u32[]{:S(2)}) copy-start(bf16[256,256]{1,0:T(8,128)(2,1)} %param.20) | copy-start | bytes 393220
  216.2 448.6 %copy-start.18 = (f32[512,256]{1,0:T(8,128)S(1)}, f32[512,256]{1,0:T(8,128)}, u32[]{:S(2)}) copy-start(f32[512,256]{1,0:T(8,128)} %get-tuple-element.38) | copy-start | bytes 1572868
  217.3 507.0 %all-to-all-start.3 = ((bf16[128,1,2,256]{3,2,1,0:T(2,128)(2,1)}), bf16[128,1,2,256]{3,2,1,0:T(2,128)(2,1)S(1)}, u32[]{:S(2)}, u32[]{:S(2)}) async-start(bf16[128,1,2,256]{3,2,1,0:T(2,128)(2,1)} %copy.38), calls=%async_computation.3 | async-start | bytes 262144 | tf_op jit(solution)/shard_map/all_to_all | solution.py:52
  224.5 496.5 %all-reduce.7.cloned.1.call-start = ((), (), s32[]{:S(2)}) async-start(), calls=%async_computation.5 | async-start | bytes 524288 | tf_op jit(solution)/shard_map/psum | solution.py:147
  726.5 5.3 copy-start.2
  (1 other events, 0.7 us)
Sparse Core Ops, SparseCore 0:
  204.9 459.8 all-reduce.4
  667.9 53.0 all-reduce.6
where the time goes:
time: 742 us
  waiting for transfers between devices  524 us (71%)
  blocking collectives  106 us (14%)
  starting transfers between devices  49.5 us (7%)
  other arithmetic  17.7 us (2%)
  local copies, waits for them, and re-layouts  16.5 us (2%)
  between operations  14.6 us (2%)
  matrix products  13.5 us (2%)
    psum x1, waiting for transfers between devices, junction_pass(): summed_rows = lax.psum(partial_value, ('len', 'pipe'))  439 us
    psum x1, blocking collectives, junction_pass(): summed_rows = lax.psum(partial_value, ('len', 'pipe'))  106 us
    psum x1, waiting for transfers between devices, body(): lax.psum(real_terms.astype(jnp.bfloat16), 'pipe').astype(jnp.float32)  54.7 us
    all_to_all x2, starting transfers between devices, to_modes(): return lax.all_to_all(field, 'len', split_axis=1, concat_axis=0, tiled=True)  26.8 us
    all_to_all x2, starting transfers between devices, from_modes(): return lax.all_to_all(field, 'len', split_axis=0, concat_axis=1, tiled=True)  22.5 us
    all_to_all x2, waiting for transfers between devices, to_modes(): return lax.all_to_all(field, 'len', split_axis=1, concat_axis=0, tiled=True)  15 us
  transfers between devices with their start and end apart: 6, of which 4 were waited for; matrix products, arithmetic and copies ran while one was open for 3% of the time, Pallas kernels for 0%

commit v1 on v0

--- a/solution.py
+++ b/solution.py
@@ -53,7 +53,7 @@
 
 
 def junction_pass(partial_value, rowwise, carried):
-    summed_rows = lax.psum(partial_value, ("len", "pipe"))
+    summed_rows = lax.psum(lax.psum(partial_value, "len"), "pipe")
     return rowwise(summed_rows, carried)
 
 

time: 742 us -> 892 us (1.20)
  waiting for transfers between devices: 524 us -> 751 us
  blocking collectives: 106 us -> 23.2 us
    psum x1 -> x3, waiting for transfers between devices: 439 us -> 676 us  [junction_pass(): summed_rows = lax.psum(lax.psum(partial_value, 'len'), 'pipe')]
    psum x1, blocking collectives: 106 us -> 23.2 us  [junction_pass(): summed_rows = lax.psum(lax.psum(partial_value, 'len'), 'pipe')]
    psum x1, waiting for transfers between devices: 54.7 us -> 43.7 us  [body(): lax.psum(real_terms.astype(jnp.bfloat16), 'pipe').astype(jnp.float32)]
  transfers between devices with their start and end apart: 6 -> 8, of which waited for: 4 -> 6; matrix products, arithmetic and copies ran while one was open for 3% -> 3% of each run, Pallas kernels for 0% -> 0%
where the time goes in v1:
time: 892 us; the launch traced here: 891 us
  waiting for transfers between devices  751 us (84%)
  starting transfers between devices  51.6 us (6%)
  blocking collectives  23.2 us (3%)
  other arithmetic  20 us (2%)
  local copies, waits for them, and re-layouts  16.6 us (2%)
  matrix products  14.4 us (2%)
  between operations  14.2 us (2%)
    psum x3, waiting for transfers between devices, junction_pass(): summed_rows = lax.psum(lax.psum(partial_value, 'len'), 'pipe')  676 us
    psum x1, waiting for transfers between devices, body(): lax.psum(real_terms.astype(jnp.bfloat16), 'pipe').astype(jnp.float32)  43.7 us
    all_to_all x2, starting transfers between devices, to_modes(): return lax.all_to_all(field, 'len', split_axis=1, concat_axis=0, tiled=True)  26.8 us
    all_to_all x2, starting transfers between devices, from_modes(): return lax.all_to_all(field, 'len', split_axis=0, concat_axis=1, tiled=True)  24.6 us
    psum x1, blocking collectives, junction_pass(): summed_rows = lax.psum(lax.psum(partial_value, 'len'), 'pipe')  23.2 us
  transfers between devices with their start and end apart: 8, of which 6 were waited for; matrix products, arithmetic and copies ran while one was open for 3% of the time, Pallas kernels for 0%

profile of v1, /device:TPU:8, one launch (start us, length us, event | category | flops | bytes accessed | tf_op | source)
XLA Modules:
  0.0 891.1 jit_solution(5229595447584517091)
XLA Ops:
  9.2 1.3 dynamic_slice.7
  12.9 4.3 negate_convert_fusion
  20.1 19.6 %all-to-all-start = ((bf16[1,128,2,256]{3,2,0,1:T(2,128)(2,1)}), bf16[1,128,2,256]{3,2,0,1:T(2,128)(2,1)S(1)}, u32[]{:S(2)}, u32[]{:S(2)}) async-start(bf16[1,128,2,256]{3,2,0,1:T(2,128)(2,1)} %bitcast.6), calls=%async_computation | async-start | bytes 262144 | tf_op jit(solution)/shard_map/all_to_all | solution.py:48
  40.3 4.4 multiply_convert_fusion.1
  47.7 301.5 %all-reduce.7.cloned.1.call-done = f32[512,256]{1,0:T(8,128)} async-done(((f32[512,256]{1,0:T(8,128)}), f32[512,256]{1,0:T(8,128)}) %all-reduce.7.cloned.1.call-update) | async-done | bytes 524304 | tf_op jit(solution)/shard_map/psum | solution.py:56
  349.2 23.2 %all-reduce.14 = bf16[512,256]{1,0:T(8,128)(2,1)S(1)} all-reduce(f32[512,256]{1,0:T(8,128)} %all-reduce.7.cloned.1.call-done), channel_id=1, replica_groups=mesh['len'=128,'pipe'=4] {'pipe'}, use_global_device_ids=true, to_apply=%region_1.2 | all-reduce | flops 131072 | bytes 786432 | tf_op jit(solution)/shard_map/psum | solution.py:56
  372.5 1.9 multiply_convert_fusion.5
  375.6 12.5 %all-to-all-start.1 = ((bf16[128,1,2,256]{3,2,1,0:T(2,128)(2,1)}), bf16[128,1,2,256]{3,2,1,0:T(2,128)(2,1)}, u32[]{:S(2)}, u32[]{:S(2)}) async-start(bf16[128,1,2,256]{3,2,1,0:T(2,128)(2,1)} %copy.34), calls=%async_computation.1 | async-start | bytes 262144 | tf_op jit(solution)/shard_map/all_to_all | solution.py:52
  388.4 16.5 %all-to-all-done.1 = bf16[128,1,2,256]{3,2,1,0:T(2,128)(2,1)} async-done(((bf16[128,1,2,256]{3,2,1,0:T(2,128)(2,1)}), bf16[128,1,2,256]{3,2,1,0:T(2,128)(2,1)}, u32[]{:S(2)}, u32[]{:S(2)}) %all-to-all-start.1) | async-done | bytes 131104 | tf_op jit(solution)/shard_map/all_to_all | solution.py:52
  407.2 3.0 convert_reduce_fusion
  412.3 7.2 all-to-all-start.2
  421.9 14.9 %all-to-all-done.2 = bf16[1,128,2,256]{3,2,0,1:T(2,128)(2,1)S(1)} async-done(((bf16[1,128,2,256]{3,2,0,1:T(2,128)(2,1)}), bf16[1,128,2,256]{3,2,0,1:T(2,128)(2,1)S(1)}, u32[]{:S(2)}, u32[]{:S(2)}) %all-to-all-start.2) | async-done | bytes 131104 | tf_op jit(solution)/shard_map/all_to_all | solution.py:48
  437.9 316.4 %all-reduce.9.cloned.1.call-done = f32[512,256]{1,0:T(8,128)} async-done(((f32[512,256]{1,0:T(8,128)}), f32[512,256]{1,0:T(8,128)}) %all-reduce.9.cloned.1.call-update) | async-done | bytes 524304 | tf_op jit(solution)/shard_map/psum | solution.py:56
  755.4 12.1 %all-to-all-start.3 = ((bf16[128,1,2,256]{3,2,1,0:T(2,128)(2,1)}), bf16[128,1,2,256]{3,2,1,0:T(2,128)(2,1)S(1)}, u32[]{:S(2)}, u32[]{:S(2)}) async-start(bf16[128,1,2,256]{3,2,1,0:T(2,128)(2,1)} %copy.38), calls=%async_computation.3 | async-start | bytes 262144 | tf_op jit(solution)/shard_map/all_to_all | solution.py:52
  767.6 43.7 %all-reduce.13.cloned.1.call-done = (bf16[1,256,256]{2,1,0:T(8,128)(2,1)}, bf16[1,256,256]{2,1,0:T(8,128)(2,1)}) async-done(((bf16[1,256,256]{2,1,0:T(8,128)(2,1)}, bf16[1,256,256]{2,1,0:T(8,128)(2,1)}), (bf16[1,256,256]{2,1,0:T(8,128)(2,1)}, bf16[1,256,256]{2,1,0:T(8,128)(2,1)})) %all-reduce.13.cloned.1.call-update) | async-done | bytes 262160 | tf_op jit(solution)/shard_map/psum | solution.py:147
  811.3 1.6 convert_element_type.176
  812.9 1.6 convert_element_type.178
  814.5 58.0 %all-reduce.11.cloned.1.call-done = f32[512,256]{1,0:T(8,128)} async-done(((f32[512,256]{1,0:T(8,128)}), f32[512,256]{1,0:T(8,128)}) %all-reduce.11.cloned.1.call-update) | async-done | bytes 524304 | tf_op jit(solution)/shard_map/psum | solution.py:56
  872.6 1.4 convolution_convert_fusion
  874.8 1.4 fusion.43
  876.3 1.8 copy.39
  878.1 1.3 scatter-add.6
  880.3 1.3 scatter-add.9
  881.6 3.0 fusion.4
  (88 shorter events, 22.8 us)
Async XLA Ops:
  7.2 399.3 %copy-start = (bf16[256,256]{1,0:T(8,128)(2,1)S(1)}, bf16[256,256]{1,0:T(8,128)(2,1)}, u32[]{:S(2)}) copy-start(bf16[256,256]{1,0:T(8,128)(2,1)} %param.16) | copy-start | bytes 393220
  7.2 342.1 %all-reduce.7.cloned.1.call-start = ((), (), s32[]{:S(2)}) async-start(), calls=%async_computation.4 | async-start | bytes 1048576 | tf_op jit(solution)/shard_map/psum | solution.py:56
  17.3 1.5 copy-start.3
  18.9 26.5 %copy-start.7 = (bf16[1,256,256]{2,1,0:T(8,128)(2,1)S(1)}, bf16[1,256,256]{2,1,0:T(8,128)(2,1)}, u32[]{:S(2)}) copy-start(bf16[1,256,256]{2,1,0:T(8,128)(2,1)} %param.19) | copy-start | bytes 393220
  20.1 354.4 %all-to-all-start = ((bf16[1,128,2,256]{3,2,0,1:T(2,128)(2,1)}), bf16[1,128,2,256]{3,2,0,1:T(2,128)(2,1)S(1)}, u32[]{:S(2)}, u32[]{:S(2)}) async-start(bf16[1,128,2,256]{3,2,0,1:T(2,128)(2,1)} %bitcast.6), calls=%async_computation | async-start | bytes 262144 | tf_op jit(solution)/shard_map/all_to_all | solution.py:48
  46.2 326.3 %copy-start.15 = (f32[256]{0:T(256)S(1)}, f32[256]{0:T(256)}, u32[]{:S(2)}) copy-start(f32[256]{0:T(256)} %param.21) | copy-start | bytes 3076
  47.7 326.8 %copy-start.9 = (bf16[1,256,256]{2,1,0:T(8,128)(2,1)S(1)}, bf16[1,256,256]{2,1,0:T(8,128)(2,1)}, u32[]{:S(2)}) copy-start(bf16[1,256,256]{2,1,0:T(8,128)(2,1)} %neg.22) | copy-start | bytes 393220
  47.7 326.7 %copy-start.12 = (bf16[1,256,256]{2,1,0:T(8,128)(2,1)S(1)}, bf16[1,256,256]{2,1,0:T(8,128)(2,1)}, u32[]{:S(2)}) copy-start(bf16[1,256,256]{2,1,0:T(8,128)(2,1)} %param.18) | copy-start | bytes 393220
  375.6 29.3 %all-to-all-start.1 = ((bf16[128,1,2,256]{3,2,1,0:T(2,128)(2,1)}), bf16[128,1,2,256]{3,2,1,0:T(2,128)(2,1)}, u32[]{:S(2)}, u32[]{:S(2)}) async-start(bf16[128,1,2,256]{3,2,1,0:T(2,128)(2,1)} %copy.34), calls=%async_computation.1 | async-start | bytes 262144 | tf_op jit(solution)/shard_map/all_to_all | solution.py:52
  388.1 18.4 %copy-start.4 = (bf16[1,2048,256]{2,1,0:T(8,128)(2,1)S(1)}, bf16[1,2048,256]{2,1,0:T(8,128)(2,1)}, u32[]{:S(2)}) copy-start(bf16[1,2048,256]{2,1,0:T(8,128)(2,1)} %param.14) | copy-start | bytes 3145732
  388.1 18.4 %copy-start.16 = (f32[256]{0:T(256)S(1)}, f32[256]{0:T(256)}, u32[]{:S(2)}) copy-start(f32[256]{0:T(256)} %param.17) | copy-start | bytes 3076
  405.9 1.2 copy-start.11
  410.2 26.6 %copy-start.6 = (bf16[16,8,2,256]{3,1,2,0:T(8,128)(2,1)S(1)}, bf16[16,8,2,256]{3,1,2,0:T(8,128)(2,1)}, u32[]{:S(2)}) copy-start(bf16[16,8,2,256]{3,1,2,0:T(8,128)(2,1)} %copy-done.5) | copy-start | bytes 393220
  412.3 24.4 %all-to-all-start.2 = ((bf16[1,128,2,256]{3,2,0,1:T(2,128)(2,1)}), bf16[1,128,2,256]{3,2,0,1:T(2,128)(2,1)S(1)}, u32[]{:S(2)}, u32[]{:S(2)}) async-start(bf16[1,128,2,256]{3,2,0,1:T(2,128)(2,1)} %bitcast.24), calls=%async_computation.2 | async-start | bytes 262144 | tf_op jit(solution)/shard_map/all_to_all | solution.py:48
  419.5 334.7 %all-reduce.9.cloned.1.call-start = ((), (), s32[]{:S(2)}) async-start(), calls=%async_computation.5 | async-start | bytes 1048576 | tf_op jit(solution)/shard_map/psum | solution.py:56
  421.8 332.5 %copy-start.8 = (bf16[1,256,256]{2,1,0:T(8,128)(2,1)S(1)}, bf16[1,256,256]{2,1,0:T(8,128)(2,1)}, u32[]{:S(2)}) copy-start(bf16[1,256,256]{2,1,0:T(8,128)(2,1)} %param.19) | copy-start | bytes 393220
  421.8 332.5 %copy-start.10 = (bf16[1,256,256]{2,1,0:T(8,128)(2,1)S(1)}, bf16[1,256,256]{2,1,0:T(8,128)(2,1)}, u32[]{:S(2)}) copy-start(bf16[1,256,256]{2,1,0:T(8,128)(2,1)} %neg.22) | copy-start | bytes 393220
  421.8 332.5 %copy-start.13 = (bf16[1,256,256]{2,1,0:T(8,128)(2,1)S(1)}, bf16[1,256,256]{2,1,0:T(8,128)(2,1)}, u32[]{:S(2)}) copy-start(bf16[1,256,256]{2,1,0:T(8,128)(2,1)} %param.18) | copy-start | bytes 393220
  421.8 389.5 %all-reduce.13.cloned.1.call-start = ((), (), s32[]{:S(2)}) async-start(), calls=%async_computation.7 | async-start | bytes 524288 | tf_op jit(solution)/shard_map/psum | solution.py:147
  437.8 434.7 %copy-start.14 = (bf16[256,256]{1,0:T(8,128)(2,1)S(1)}, bf16[256,256]{1,0:T(8,128)(2,1)}, u32[]{:S(2)}) copy-start(bf16[256,256]{1,0:T(8,128)(2,1)} %param.20) | copy-start | bytes 393220
  437.8 434.7 %copy-start.17 = (f32[512,256]{1,0:T(8,128)S(1)}, f32[512,256]{1,0:T(8,128)}, u32[]{:S(2)}) copy-start(f32[512,256]{1,0:T(8,128)} %get-tuple-element.38) | copy-start | bytes 1572868
  437.9 434.7 %all-reduce.11.cloned.1.call-start = ((), (), s32[]{:S(2)}) async-start(), calls=%async_computation.6 | async-start | bytes 1048576 | tf_op jit(solution)/shard_map/psum | solution.py:56
  755.4 118.7 %all-to-all-start.3 = ((bf16[128,1,2,256]{3,2,1,0:T(2,128)(2,1)}), bf16[128,1,2,256]{3,2,1,0:T(2,128)(2,1)S(1)}, u32[]{:S(2)}, u32[]{:S(2)}) async-start(bf16[128,1,2,256]{3,2,1,0:T(2,128)(2,1)} %copy.38), calls=%async_computation.3 | async-start | bytes 262144 | tf_op jit(solution)/shard_map/all_to_all | solution.py:52
  876.3 5.3 copy-start.2
  (2 other events, 2.1 us)
Sparse Core Ops, SparseCore 0:
  13.0 336.1 all-reduce.6
  424.2 330.0 all-reduce.8
  757.3 53.9 all-reduce.12
  813.6 58.8 all-reduce.10
